TPU v7x, 32 devices: a whole 2x2x4 slice. The times are simulated.
32 devices in a mesh: grp: 2 (over x), beam: 16 (over z, y, core).
Axes of the slice: x: 2, y: 2, z: 4, core: 2. Of those that a mesh axis runs over, the one named last changes fastest.
Arguments:
- s_matrix: bfloat16 [2, 2048, 16, 4096], P(None, ('grp', 'beam')), parts along dimension 1, may hold values from -6 to 6
- beam_weight: float32 [2, 2048], P(None, ('grp', 'beam')), parts along dimension 1, may hold values from -0.25 to 0.25
- probe_shift: int32 [256, 2], P(('grp', 'beam')), parts along dimension 0, may hold values from 0 to 191
- probe_cutoff: int32 [256], P(('grp', 'beam')), parts along dimension 0, may hold values from 64 to 512
- target: bfloat16 [2, 256, 4096], P(None, ('grp', 'beam')), parts along dimension 1, may hold values from -3 to 3
- target_exp: int32 [256], P(('grp', 'beam')), parts along dimension 0, may hold values from -1 to 2
Outputs:
- s_grad: bfloat16 [2, 2048, 16, 4096], P(None, ('grp', 'beam')), parts along dimension 1
There are 2 independent parts, one for each index of `grp`. A program takes and returns all parts, laid end to end along the dimension named above; each array names one. Nothing has to cross between parts.
All inputs are finite; a program needn't handle non-finite values.
Results may differ from a plain program's by a relative error of at most 0.006.
Values may be sent and summed in bfloat16 or wider, within the bound.
A program may use at most 128 MiB of HBM per device.

v0:
```python
import functools
import math

import jax
import jax.numpy as jnp
from jax import lax
from jax.experimental import pallas as pl
from jax.experimental.pallas import tpu as pltpu
from jax.sharding import PartitionSpec as P

SIDE = 32
GRID = 192
TILE_SIDE = 4
TWO_PI = 2.0 * math.pi
CHUNKS = 8
SWAP = True
GAP_NEAR = 2
GAP_FAR = 4
MATMUL_COLUMNS = 512


def stage_strides(n):
    return [2**k for k in range(n.bit_length() - 1)]


def orders(n):
    strides = stage_strides(n)
    other = list(strides)
    if SWAP and len(other) > 2:
        other[1], other[2] = other[2], other[1]
    return strides, other


def place(me, strides, unit, upto):
    levels = len(strides)
    base = 0
    for k in range(upto):
        base = base + (me // strides[k]) % 2 * (unit * 2 ** (levels - 1 - k))
    return base


def wave_kernel(
    n, local, tile_count, pixels, strides, other,
    par_ref, weight_ref, target_ref, s_ref,
    res_ref, left_ref,
    pars, s_vmem, acc, sbuf, rbuf, mixed_left, mixed_res,
    par_send, par_recv, s_sem, send_sem, recv_sem,
):
    levels = len(strides)
    me = lax.axis_index("beam")
    unit = par_ref.shape[0]
    rows = n * unit
    width = local * tile_count
    wide = pixels // CHUNKS

    def order(c):
        return other if c % 2 else strides

    moves = [(place(i, other, unit, levels), place(i, strides, unit, levels)) for i in range(n)]

    def partner(stride):
        return me + (1 - 2 * ((me // stride) % 2)) * stride

    def columns(c):
        return pl.ds(c * wide, wide)

    loads = []
    for c in range(CHUNKS):
        load = pltpu.make_async_copy(s_ref.at[:, columns(c)], s_vmem.at[:, columns(c)], s_sem.at[c])
        load.start()
        loads.append(load)

    barrier = pltpu.get_barrier_semaphore()
    for ahead in range(1, n):
        pl.semaphore_signal(
            barrier, inc=1, device_id={"beam": lax.rem(me + ahead, n)}, device_id_type=pl.DeviceIdType.MESH
        )
    pl.semaphore_wait(barrier, n - 1)

    sent = []

    def send(source, target, send_semaphore, recv_semaphore, peer):
        copy = pltpu.make_async_remote_copy(
            src_ref=source,
            dst_ref=target,
            send_sem=send_semaphore,
            recv_sem=recv_semaphore,
            device_id={"beam": peer},
            device_id_type=pl.DeviceIdType.MESH,
        )
        copy.start()
        sent.append(copy)
        return copy

    def mine(k, steps=strides):
        size = unit * 2 ** (levels - k)
        return pl.ds(pl.multiple_of(place(me, steps, unit, k), size), size)

    pars[mine(levels), :] = par_ref[...]
    asked = [
        send(par_ref, pars.at[mine(levels), :], par_send.at[ahead - 1], par_recv.at[ahead - 1], lax.rem(me + ahead, n))
        for ahead in range(1, n)
    ]
    for copy in asked:
        copy.wait_recv()

    half = SIDE // 2
    beam = me * local + lax.broadcasted_iota(jnp.int32, (1, local), 1)
    freq_x = beam % SIDE - half
    freq_y = beam // SIDE - half
    shift_x = pars[:, 0:1]
    shift_y = pars[:, 1:2]
    cutoff = pars[:, 2:3]
    ramp = (freq_x * shift_x + freq_y * shift_y) % GRID
    phase = ramp.astype(jnp.float32) * (TWO_PI / GRID)
    inside = (freq_x * freq_x + freq_y * freq_y) <= cutoff
    cosine = jnp.cos(phase)
    sine = jnp.sin(phase)
    w_real = weight_ref[0:1, :]
    w_imag = weight_ref[1:2, :]
    c_real = jnp.where(inside, w_real * cosine + w_imag * sine, 0.0)
    c_imag = jnp.where(inside, w_imag * cosine - w_real * sine, 0.0)
    is_real = lax.broadcasted_iota(jnp.int32, (rows, 1), 0) % unit < unit // 2
    first = jnp.where(is_real, c_real, c_imag).astype(jnp.bfloat16)
    second = jnp.where(is_real, -c_imag, c_real).astype(jnp.bfloat16)
    step = GRID // TILE_SIDE
    window = shift_x // step * TILE_SIDE + shift_y // step
    place_of = lax.broadcasted_iota(jnp.int32, (1, width), 1)
    chosen = window == place_of % tile_count
    spread = lax.broadcasted_iota(jnp.int32, (local, width), 1) // tile_count
    spread = (spread == lax.broadcasted_iota(jnp.int32, (local, width), 0)).astype(jnp.float32).astype(jnp.bfloat16)
    for at, part in ((0, first), (width, second)):
        full = jnp.dot(part, spread, preferred_element_type=jnp.float32)
        left_ref[:, at : at + width] = jnp.where(chosen, full, 0.0).astype(jnp.bfloat16)

    if other != strides:
        for at, old in moves:
            mixed_left[at : at + unit, :] = left_ref[old : old + unit, :]

    def left_of(c):
        return left_ref if order(c) == strides else mixed_left

    def res_of(c):
        return res_ref if order(c) == strides else mixed_res

    narrow = min(MATMUL_COLUMNS, wide)

    def multiply(c):
        def tile(i, carry):
            at = pl.ds(pl.multiple_of(c * wide + i * narrow, narrow), narrow)
            acc[:, at] = jnp.dot(left_of(c)[...], s_vmem[:, at], preferred_element_type=jnp.float32)
            return carry

        lax.fori_loop(0, wide // narrow, tile, 0)

    def scatter_rows(c, k):
        size = rows // 2 ** (k + 1)
        base = place(me, order(c), unit, k)
        bit = (me // order(c)[k]) % 2
        keep = pl.ds(pl.multiple_of(base + bit * size, size), size)
        give = pl.ds(pl.multiple_of(base + (1 - bit) * size, size), size)
        slot = pl.ds(rows - 2 * size, size)
        return keep, give, slot

    def start_scatter(c, k):
        _, give, slot = scatter_rows(c, k)
        sbuf[slot, columns(c)] = acc[give, columns(c)].astype(jnp.bfloat16)
        return send(
            sbuf.at[slot, columns(c)],
            rbuf.at[slot, columns(c)],
            send_sem.at[c, k],
            recv_sem.at[c, k],
            partner(order(c)[k]),
        )

    def end_scatter(c, k):
        keep, _, slot = scatter_rows(c, k)
        acc[keep, columns(c)] += rbuf[slot, columns(c)].astype(jnp.float32)

    def residual(c):
        own = mine(levels, order(c))
        scale = jnp.exp2(par_ref[:, 3:4].astype(jnp.float32))
        goal = target_ref[:, columns(c)].astype(jnp.float32) * scale
        res_of(c)[own, columns(c)] = (acc[own, columns(c)] - goal).astype(jnp.bfloat16)

    def start_gather(c, k):
        held = res_of(c).at[mine(k + 1, order(c)), columns(c)]
        at = 2 * levels - 1 - k
        return send(held, held, send_sem.at[c, at], recv_sem.at[c, at], partner(order(c)[k]))

    def slots(c):
        hops = order(c) + order(c)[::-1]
        taken = [0]
        for stride in hops:
            taken.append(taken[-1] + (GAP_NEAR if stride == 1 else GAP_FAR))
        return taken

    flight = {}
    for time in range(CHUNKS + slots(0)[-1]):
        for c in range(CHUNKS):
            if time - c not in slots(c):
                continue
            at = slots(c).index(time - c)
            if at == 0:
                loads[c].wait()
                multiply(c)
            else:
                flight[c].wait_recv()
                if at <= levels:
                    end_scatter(c, at - 1)
            if at < levels:
                flight[c] = start_scatter(c, at)
            elif at < 2 * levels:
                if at == levels:
                    residual(c)
                flight[c] = start_gather(c, 2 * levels - 1 - at)
    for c in range(CHUNKS):
        if order(c) != strides:
            for at, old in moves:
                res_ref[old : old + unit, columns(c)] = mixed_res[at : at + unit, columns(c)]
    for copy in sent:
        copy.wait_send()


def grad_kernel(left_ref, res_ref, out_ref):
    dims = (((0,), (0,)), ((), ()))
    out_ref[...] = lax.dot_general(left_ref[...], res_ref[...], dims, preferred_element_type=jnp.float32).astype(
        out_ref.dtype
    )


def body(n, s_matrix, beam_weight, probe_shift, probe_cutoff, target, target_exp):
    _, local, tile_count, pixels = s_matrix.shape
    probes = probe_shift.shape[0]
    strides, other = orders(n)
    levels = len(strides)
    unit = 2 * probes
    rows = n * unit
    width = local * tile_count
    pars = jnp.concatenate([probe_shift, probe_cutoff[:, None], target_exp[:, None]], axis=1)
    pars = jnp.pad(jnp.concatenate([pars, pars], axis=0), ((0, 0), (0, 124)))
    vmem = pl.BlockSpec(memory_space=pltpu.VMEM)
    res, left = pl.pallas_call(
        functools.partial(wave_kernel, n, local, tile_count, pixels, strides, other),
        out_shape=(
            jax.ShapeDtypeStruct((rows, pixels), jnp.bfloat16),
            jax.ShapeDtypeStruct((rows, 2 * width), jnp.bfloat16),
        ),
        in_specs=[vmem, vmem, vmem, pl.BlockSpec(memory_space=pl.ANY)],
        out_specs=(vmem, vmem),
        scratch_shapes=[
            pltpu.VMEM((rows, 128), jnp.int32),
            pltpu.VMEM((2 * width, pixels), jnp.bfloat16),
            pltpu.VMEM((rows, pixels), jnp.float32),
            pltpu.VMEM((rows, pixels), jnp.bfloat16),
            pltpu.VMEM((rows, pixels), jnp.bfloat16),
            pltpu.VMEM((rows, 2 * width), jnp.bfloat16),
            pltpu.VMEM((rows, pixels), jnp.bfloat16),
            pltpu.SemaphoreType.DMA((n - 1,)),
            pltpu.SemaphoreType.DMA((n - 1,)),
            pltpu.SemaphoreType.DMA((CHUNKS,)),
            pltpu.SemaphoreType.DMA((CHUNKS, 2 * levels)),
            pltpu.SemaphoreType.DMA((CHUNKS, 2 * levels)),
        ],
        compiler_params=pltpu.CompilerParams(
            collective_id=0, has_side_effects=True, vmem_limit_bytes=60 * 2**20
        ),
    )(pars, beam_weight, target.reshape(unit, pixels), s_matrix.reshape(2 * width, pixels))
    tall = min(512, width)
    grad = pl.pallas_call(
        grad_kernel,
        grid=(2 * width // tall,),
        out_shape=jax.ShapeDtypeStruct((2 * width, pixels), jnp.bfloat16),
        in_specs=[
            pl.BlockSpec((rows, tall), lambda i: (0, i)),
            pl.BlockSpec((rows, pixels), lambda i: (0, 0)),
        ],
        out_specs=pl.BlockSpec((tall, pixels), lambda i: (i, 0)),
        compiler_params=pltpu.CompilerParams(vmem_limit_bytes=60 * 2**20),
    )(left, res)
    return grad.reshape(2, local, tile_count, pixels)


def solution(mesh):
    return jax.shard_map(
        functools.partial(body, mesh.shape["beam"]),
        mesh=mesh,
        in_specs=(
            P(None, ("grp", "beam"), None, None),
            P(None, ("grp", "beam")),
            P(("grp", "beam"), None),
            P(("grp", "beam")),
            P(None, ("grp", "beam"), None),
            P(("grp", "beam")),
        ),
        out_specs=P(None, ("grp", "beam"), None, None),
        check_vma=False,
    )
```

profile of v0, /device:TPU:0, one launch (start us, length us, event | category | flops | bytes accessed | tf_op | source)
XLA Modules:
  0.0 60.4 jit_solution(6843019539188443384)
XLA Ops:
  0.0 0.8 %add_add_fusion = s32[16,4]{0,1:T(4,128)S(1)} fusion(s32[8,1]{0,1:T(1,128)} %bitcast.7, s32[8,1]{0,1:T(1,128)} %bitcast.8, s32[8,2]{0,1:T(2,128)} %param.8), kind=kLoop, calls=%fused_computation | loop fusion | flops 320 | bytes 384 | tf_op jit(solution)/shard_map/concatenate | solution.py:241
  0.8 0.1 copy.10
  0.9 0.6 %pad.4.par_ref = s32[16,128]{1,0:T(8,128)} pad(s32[16,4]{1,0:T(8,128)S(1)} %copy.10, s32[]{:T(128)} %constant.0.clone.1), padding=0_0x0_124 | pad | bytes 8452 | tf_op jit(solution)/shard_map/jit(_pad)/pad | solution.py:241
  1.5 49.2 %shard_map.64 = (bf16[256,4096]{1,0:T(8,128)(2,1)}, bf16[256,2048]{1,0:T(8,128)(2,1)}) custom-call(s32[16,128]{1,0:T(8,128)} %pad.4.par_ref, f32[2,64]{1,0:T(2,128)} %weight_ref.1, bf16[16,4096]{1,0:T(8,128)(2,1)} %bitcast.6, bf16[2048,4096]{1,0:T(8,128)(2,1)} %bitcast.5), custom_call_target="tpu_custom_call" | custom-call | tf_op jit(solution)/shard_map/pallas_call | solution.py:243
  50.7 9.7 %shard_map.65 = bf16[2048,4096]{1,0:T(8,128)(2,1)} custom-call(bf16[256,2048]{1,0:T(8,128)(2,1)} %get-tuple-element.7.left_ref, bf16[256,4096]{1,0:T(8,128)(2,1)} %get-tuple-element.8.res_ref), custom_call_target="tpu_custom_call" | custom-call | tf_op jit(solution)/shard_map/pallas_call | solution.py:270
where the time goes:
time: 60.7 us; the launch traced here: 60.4 us
  Pallas kernels  58.9 us (97%)
  other arithmetic  0.84 us (1%)
  local copies, waits for them, and re-layouts  0.69 us (1%)
    pallas_call x1, Pallas kernels, body(): pl.pallas_call(functools.partial(wave_kernel, n, local, tile_count, pixel...  49.2 us
    pallas_call x1, Pallas kernels, body(): pl.pallas_call(grad_kernel, grid=(2 * width // tall,), out_shape=jax.Shap...  9.67 us

commit v1 on v0

--- a/solution.py
+++ b/solution.py
@@ -19,54 +19,126 @@
 MATMUL_COLUMNS = 512
 
 
-def stage_strides(n):
-    return [2**k for k in range(n.bit_length() - 1)]
-
-
-def orders(n):
-    strides = stage_strides(n)
-    other = list(strides)
-    if SWAP and len(other) > 2:
-        other[1], other[2] = other[2], other[1]
-    return strides, other
-
-
-def place(me, strides, unit, upto):
-    levels = len(strides)
-    base = 0
-    for k in range(upto):
-        base = base + (me // strides[k]) % 2 * (unit * 2 ** (levels - 1 - k))
-    return base
-
-
-def wave_kernel(
-    n, local, tile_count, pixels, strides, other,
+KINDS = ("YY",) * 8
+LINK_RATE = 46.5e3
+CORE_RATE = 250e3
+LINK_LAG = 1.66
+CORE_LAG = 0.9
+PRODUCT_US = 5.5
+ADD_US = 0.3
+NAMES = ("r1", "r2", "r3f", "r3n", "r4", "ga", "gb", "gn1", "gn2", "gf1", "gf2", "ac")
+
+
+def steps_of(inner, kind):
+    sums, spread = kind
+    steps = [("M", (), (("c", "r1", 4),), 0, ())]
+    if spread == "Y":
+        first = (("m", "gf1", 1), ("o", "gn1", 1), ("y", "ga", 1))
+    else:
+        first = (("y", "ga", 1), ("m", "gf1", 1), ("o", "gn1", 1))
+    edge_sums = (("t", "r3f", 1), ("t", "r3n", 1)) if sums == "Y" else (("t", "r3f", 2), ("t", "r3n", 2))
+    if sums == "Y":
+        steps.append(("C", ("r1",), (("y", "r2", 2),), 4, ("M",)))
+        if inner:
+            steps.append(("Y", ("r2",), (), 2, ("C",)))
+            steps.append(("F", ("r3f",), (("m", "r4", 1),), 1, ("Y",)))
+            steps.append(("N", ("r3n", "r4"), first, 1, ("F",)))
+        else:
+            steps.append(("Y", ("r2",), edge_sums, 2, ("C",)))
+        last = "N"
+    else:
+        if inner:
+            steps.append(("C", ("r1",), (), 4, ("M",)))
+            steps.append(("F", ("r3f",), (("m", "r4", 2),), 2, ("C",)))
+            steps.append(("N", ("r3n", "r4"), (("y", "r2", 1),), 2, ("F",)))
+            steps.append(("Y", ("r2",), first, 1, ("N",)))
+        else:
+            steps.append(("C", ("r1",), edge_sums, 4, ("M",)))
+        last = "Y"
+    if spread == "Y":
+        if inner:
+            steps.append(("G1", ("gf1",), (("o", "gf1", 1), ("y", "gb", 1)), 0, ()))
+            steps.append(("A", ("ga", "gb"), (("c", "ac", 4),), 0, (last, "G1")))
+        else:
+            steps.append(("G1", ("gn1",), (("y", "ga", 1),), 0, ()))
+            steps.append(("G2", ("gf1",), (("y", "gb", 1),), 0, ()))
+            steps.append(("A", ("ga", "gb"), (("c", "ac", 4),), 0, ("G1", "G2")))
+    elif inner:
+        steps.append(("H", ("ga",), (("m", "gf2", 1), ("o", "gn2", 1)), 0, ()))
+        steps.append(("G1", ("gf1",), (("o", "gf1", 1),), 0, ()))
+        steps.append(("A", ("gf2",), (("o", "gf2", 1), ("c", "ac", 4)), 0, (last, "H", "G1")))
+    else:
+        steps.append(("A", ("gn1", "gn2", "gf1", "gf2"), (("c", "ac", 4),), 0, ()))
+    steps.append(("E", ("ac",), (), 0, ()))
+    return steps
+
+
+def schedule(block_bytes):
+    chunks = len(KINDS)
+    waiting = [[(k, step) for k in range(chunks) for step in steps_of(inner, KINDS[k])] for inner in (False, True)]
+    arrived, done = ({}, {}), ({}, {})
+    free, links = [0.0, 0.0], {}
+    order = ([], [])
+    while waiting[0] or waiting[1]:
+        best = None
+        for role in (0, 1):
+            for k, step in waiting[role]:
+                name, needs, _, _, after = step
+                if name == "M" and k > 0 and (k - 1, "M") not in done[role]:
+                    continue
+                if any((k, x) not in arrived[role] for x in needs) or any((k, x) not in done[role] for x in after):
+                    continue
+                ready = max([free[role]] + [arrived[role][k, x] for x in needs])
+                rank = (ready, name == "M", k, role, name)
+                if best is None or rank < best[0]:
+                    best = (rank, role, k, step)
+        (ready, *_), role, k, step = best
+        name, _, sends, blocks, _ = step
+        end = ready + (PRODUCT_US if name == "M" else 0.02 * chunks + ADD_US * blocks) / chunks
+        free[role] = end
+        done[role][k, name] = end
+        waiting[role].remove((k, step))
+        order[role].append((k, name))
+        for link, message, count in sends:
+            rate, lag = (CORE_RATE, CORE_LAG) if link == "c" else (LINK_RATE, LINK_LAG)
+            sent = max(end, links.get((role, link), 0.0)) + count * block_bytes / rate
+            links[role, link] = sent
+            arrived[{"t": 1, "o": 0}.get(link, role)][k, message] = sent + lag
+    return order
+
+
+def grid_kernel(
+    n, local, tile_count, pixels,
     par_ref, weight_ref, target_ref, s_ref,
     res_ref, left_ref,
-    pars, s_vmem, acc, sbuf, rbuf, mixed_left, mixed_res,
+    pars, s_vmem, acc, sbuf, r1, r2, r3, r4,
     par_send, par_recv, s_sem, send_sem, recv_sem,
 ):
-    levels = len(strides)
     me = lax.axis_index("beam")
     unit = par_ref.shape[0]
     rows = n * unit
     width = local * tile_count
-    wide = pixels // CHUNKS
-
-    def order(c):
-        return other if c % 2 else strides
-
-    moves = [(place(i, other, unit, levels), place(i, strides, unit, levels)) for i in range(n)]
-
-    def partner(stride):
-        return me + (1 - 2 * ((me // stride) % 2)) * stride
-
-    def columns(c):
-        return pl.ds(c * wide, wide)
+    chunks = len(KINDS)
+    wide = pixels // chunks
+    block = rows // 8
+    core, across, line = me % 2, me // 2 % 2, me // 4
+    side = line // 2
+    far = 1 - side
+    inward = (1 - 2 * side) * 4
+    peers = {
+        "c": me + 1 - 2 * core,
+        "y": me + 2 - 4 * across,
+        "t": me + inward,
+        "m": me + inward,
+        "o": me - inward,
+    }
+
+    def columns(k):
+        return pl.ds(k * wide, wide)
 
     loads = []
-    for c in range(CHUNKS):
-        load = pltpu.make_async_copy(s_ref.at[:, columns(c)], s_vmem.at[:, columns(c)], s_sem.at[c])
+    for k in range(chunks):
+        load = pltpu.make_async_copy(s_ref.at[:, columns(k)], s_vmem.at[:, columns(k)], s_sem.at[k])
         load.start()
         loads.append(load)
 
@@ -77,10 +149,8 @@
         )
     pl.semaphore_wait(barrier, n - 1)
 
-    sent = []
-
-    def send(source, target, send_semaphore, recv_semaphore, peer):
-        copy = pltpu.make_async_remote_copy(
+    def remote(source, target, send_semaphore, recv_semaphore, peer):
+        return pltpu.make_async_remote_copy(
             src_ref=source,
             dst_ref=target,
             send_sem=send_semaphore,
@@ -88,19 +158,15 @@
             device_id={"beam": peer},
             device_id_type=pl.DeviceIdType.MESH,
         )
-        copy.start()
-        sent.append(copy)
-        return copy
-
-    def mine(k, steps=strides):
-        size = unit * 2 ** (levels - k)
-        return pl.ds(pl.multiple_of(place(me, steps, unit, k), size), size)
-
-    pars[mine(levels), :] = par_ref[...]
+
+    mine = pl.ds(pl.multiple_of(me * unit, unit), unit)
+    pars[mine, :] = par_ref[...]
     asked = [
-        send(par_ref, pars.at[mine(levels), :], par_send.at[ahead - 1], par_recv.at[ahead - 1], lax.rem(me + ahead, n))
+        remote(par_ref, pars.at[mine, :], par_send.at[ahead - 1], par_recv.at[ahead - 1], lax.rem(me + ahead, n))
         for ahead in range(1, n)
     ]
+    for copy in asked:
+        copy.start()
     for copy in asked:
         copy.wait_recv()
 
@@ -133,6 +199,269 @@
         full = jnp.dot(part, spread, preferred_element_type=jnp.float32)
         left_ref[:, at : at + width] = jnp.where(chosen, full, 0.0).astype(jnp.bfloat16)
 
+    own = (me * unit // block // 4, me * unit // block // 2 % 2, me * unit // block % 2)
+    own_rows = pl.ds(pl.multiple_of(me * unit % block, unit), unit)
+
+    def run(inner, steps):
+        sent = []
+
+        def send(k, link, message, source, target):
+            copy = remote(
+                source, target, send_sem.at[k, len([1 for other, _ in sent if other == k])],
+                recv_sem.at[k, NAMES.index(message)], peers[link],
+            )
+            copy.start()
+            sent.append((k, copy))
+
+        def got(k, message, view):
+            remote(view, view, send_sem.at[k, 0], recv_sem.at[k, NAMES.index(message)], peers["c"]).wait_recv()
+
+        def low(x):
+            return x.astype(jnp.bfloat16)
+
+        def spread_first(k):
+            held = res_ref.at[k, core, across, side]
+            if KINDS[k][1] == "Y":
+                send(k, "m", "gf1", held, held)
+                send(k, "o", "gn1", held, held)
+                send(k, "y", "ga", held, held)
+            else:
+                send(k, "y", "ga", held, held)
+                send(k, "m", "gf1", held, held)
+                send(k, "o", "gn1", held, held)
+
+        def take(k, name):
+            by_y = KINDS[k][0] == "Y"
+            at = (k, core, across)
+            here = (k, core, across, side)
+            if name == "M":
+                loads[k].wait()
+                product = jnp.dot(left_ref[...], s_vmem[:, columns(k)], preferred_element_type=jnp.float32)
+                acc[k] = product.reshape(2, 2, 2, block, wide)
+                goal = target_ref[:, columns(k)].astype(jnp.float32) * jnp.exp2(par_ref[:, 3:4].astype(jnp.float32))
+                acc[(k, *own, own_rows)] = acc[(k, *own, own_rows)] - goal
+                sbuf[k, 1 - core] = low(acc[k, 1 - core])
+                send(k, "c", "r1", sbuf.at[k, 1 - core], r1.at[k])
+            elif name == "C":
+                got(k, "r1", r1.at[k])
+                if by_y:
+                    sbuf[k, core, 1 - across] = low(acc[k, core, 1 - across] + r1[k, 1 - across].astype(jnp.float32))
+                    send(k, "y", "r2", sbuf.at[k, core, 1 - across], r2.at[k])
+                    acc[at] = acc[at] + r1[k, across].astype(jnp.float32)
+                elif inner:
+                    acc[k, core] = acc[k, core] + r1[k].astype(jnp.float32)
+                else:
+                    for at_side, message, slot in ((far, "r3f", 0), (side, "r3n", 1)):
+                        total = acc[k, core, :, at_side] + r1[k, :, at_side].astype(jnp.float32)
+                        sbuf[k, core, :, at_side] = low(total)
+                        send(k, "t", message, sbuf.at[k, core, :, at_side], r3.at[k, slot])
+            elif name == "Y":
+                if by_y:
+                    got(k, "r2", r2.at[k])
+                    total = acc[at] + r2[k].astype(jnp.float32)
+                    if inner:
+                        acc[at] = total
+                    else:
+                        sbuf[at] = low(total)
+                        send(k, "t", "r3f", sbuf.at[(*at, far)], r3.at[k, 0, 0])
+                        send(k, "t", "r3n", sbuf.at[(*at, side)], r3.at[k, 1, 0])
+                else:
+                    got(k, "r2", r2.at[k, 0])
+                    res_ref[here] = low(acc[here] + r2[k, 0].astype(jnp.float32))
+                    spread_first(k)
+            elif name == "F":
+                if by_y:
+                    got(k, "r3f", r3.at[k, 0, 0])
+                    sbuf[(*at, far)] = low(acc[(*at, far)] + r3[k, 0, 0].astype(jnp.float32))
+                    send(k, "m", "r4", sbuf.at[(*at, far)], r4.at[k, 0])
+                else:
+                    got(k, "r3f", r3.at[k, 0])
+                    sbuf[k, core, :, far] = low(acc[k, core, :, far] + r3[k, 0].astype(jnp.float32))
+                    send(k, "m", "r4", sbuf.at[k, core, :, far], r4.at[k])
+            elif name == "N":
+                if by_y:
+                    got(k, "r3n", r3.at[k, 1, 0])
+                    got(k, "r4", r4.at[k, 0])
+                    total = acc[here] + r3[k, 1, 0].astype(jnp.float32) + r4[k, 0].astype(jnp.float32)
+                    res_ref[here] = low(total)
+                    spread_first(k)
+                else:
+                    got(k, "r3n", r3.at[k, 1])
+                    got(k, "r4", r4.at[k])
+                    there = (k, core, 1 - across, side)
+                    total = acc[there] + r3[k, 1, 1 - across].astype(jnp.float32) + r4[k, 1 - across].astype(jnp.float32)
+                    sbuf[there] = low(total)
+                    send(k, "y", "r2", sbuf.at[there], r2.at[k, 0])
+                    acc[here] = acc[here] + r3[k, 1, across].astype(jnp.float32) + r4[k, across].astype(jnp.float32)
+            elif name == "A":
+                if KINDS[k][1] == "Y":
+                    got(k, "ga", res_ref.at[here])
+                    got(k, "gb", res_ref.at[here])
+                elif inner:
+                    got(k, "gf2", res_ref.at[here])
+                    held = res_ref.at[k, core, 1 - across, far]
+                    send(k, "o", "gf2", held, held)
+                else:
+                    for message in ("gn1", "gn2", "gf1", "gf2"):
+                        got(k, message, res_ref.at[here])
+                send(k, "c", "ac", res_ref.at[k, core], res_ref.at[k, core])
+            elif name == "H":
+                got(k, "ga", res_ref.at[here])
+                held = res_ref.at[k, core, 1 - across, side]
+                send(k, "m", "gf2", held, held)
+                send(k, "o", "gn2", held, held)
+            elif name == "G1":
+                if inner:
+                    got(k, "gf1", res_ref.at[here])
+                    held = res_ref.at[(*at, far)]
+                    send(k, "o", "gf1", held, held)
+                    if KINDS[k][1] == "Y":
+                        send(k, "y", "gb", held, held)
+                else:
+                    got(k, "gn1", res_ref.at[here])
+                    held = res_ref.at[here]
+                    send(k, "y", "ga", held, held)
+            elif name == "G2":
+                got(k, "gf1", res_ref.at[here])
+                held = res_ref.at[(*at, far)]
+                send(k, "y", "gb", held, held)
+            elif name == "E":
+                got(k, "ac", res_ref.at[k, 1 - core])
+
+        for k, name in steps:
+            take(k, name)
+        for _, copy in sent:
+            copy.wait_send()
+
+    edge_steps, inner_steps = schedule(block * wide * 2)
+    middle = (line == 1) | (line == 2)
+
+    @pl.when(middle)
+    def _():
+        run(True, inner_steps)
+
+    @pl.when(jnp.logical_not(middle))
+    def _():
+        run(False, edge_steps)
+
+    for copy in asked:
+        copy.wait_send()
+
+
+def stage_strides(n):
+    return [2**k for k in range(n.bit_length() - 1)]
+
+
+def orders(n):
+    strides = stage_strides(n)
+    other = list(strides)
+    if SWAP and len(other) > 2:
+        other[1], other[2] = other[2], other[1]
+    return strides, other
+
+
+def place(me, strides, unit, upto):
+    levels = len(strides)
+    base = 0
+    for k in range(upto):
+        base = base + (me // strides[k]) % 2 * (unit * 2 ** (levels - 1 - k))
+    return base
+
+
+def wave_kernel(
+    n, local, tile_count, pixels, strides, other,
+    par_ref, weight_ref, target_ref, s_ref,
+    res_ref, left_ref,
+    pars, s_vmem, acc, sbuf, rbuf, mixed_left, mixed_res,
+    par_send, par_recv, s_sem, send_sem, recv_sem,
+):
+    levels = len(strides)
+    me = lax.axis_index("beam")
+    unit = par_ref.shape[0]
+    rows = n * unit
+    width = local * tile_count
+    wide = pixels // CHUNKS
+
+    def order(c):
+        return other if c % 2 else strides
+
+    moves = [(place(i, other, unit, levels), place(i, strides, unit, levels)) for i in range(n)]
+
+    def partner(stride):
+        return me + (1 - 2 * ((me // stride) % 2)) * stride
+
+    def columns(c):
+        return pl.ds(c * wide, wide)
+
+    loads = []
+    for c in range(CHUNKS):
+        load = pltpu.make_async_copy(s_ref.at[:, columns(c)], s_vmem.at[:, columns(c)], s_sem.at[c])
+        load.start()
+        loads.append(load)
+
+    barrier = pltpu.get_barrier_semaphore()
+    for ahead in range(1, n):
+        pl.semaphore_signal(
+            barrier, inc=1, device_id={"beam": lax.rem(me + ahead, n)}, device_id_type=pl.DeviceIdType.MESH
+        )
+    pl.semaphore_wait(barrier, n - 1)
+
+    sent = []
+
+    def send(source, target, send_semaphore, recv_semaphore, peer):
+        copy = pltpu.make_async_remote_copy(
+            src_ref=source,
+            dst_ref=target,
+            send_sem=send_semaphore,
+            recv_sem=recv_semaphore,
+            device_id={"beam": peer},
+            device_id_type=pl.DeviceIdType.MESH,
+        )
+        copy.start()
+        sent.append(copy)
+        return copy
+
+    def mine(k, steps=strides):
+        size = unit * 2 ** (levels - k)
+        return pl.ds(pl.multiple_of(place(me, steps, unit, k), size), size)
+
+    pars[mine(levels), :] = par_ref[...]
+    asked = [
+        send(par_ref, pars.at[mine(levels), :], par_send.at[ahead - 1], par_recv.at[ahead - 1], lax.rem(me + ahead, n))
+        for ahead in range(1, n)
+    ]
+    for copy in asked:
+        copy.wait_recv()
+
+    half = SIDE // 2
+    beam = me * local + lax.broadcasted_iota(jnp.int32, (1, local), 1)
+    freq_x = beam % SIDE - half
+    freq_y = beam // SIDE - half
+    shift_x = pars[:, 0:1]
+    shift_y = pars[:, 1:2]
+    cutoff = pars[:, 2:3]
+    ramp = (freq_x * shift_x + freq_y * shift_y) % GRID
+    phase = ramp.astype(jnp.float32) * (TWO_PI / GRID)
+    inside = (freq_x * freq_x + freq_y * freq_y) <= cutoff
+    cosine = jnp.cos(phase)
+    sine = jnp.sin(phase)
+    w_real = weight_ref[0:1, :]
+    w_imag = weight_ref[1:2, :]
+    c_real = jnp.where(inside, w_real * cosine + w_imag * sine, 0.0)
+    c_imag = jnp.where(inside, w_imag * cosine - w_real * sine, 0.0)
+    is_real = lax.broadcasted_iota(jnp.int32, (rows, 1), 0) % unit < unit // 2
+    first = jnp.where(is_real, c_real, c_imag).astype(jnp.bfloat16)
+    second = jnp.where(is_real, -c_imag, c_real).astype(jnp.bfloat16)
+    step = GRID // TILE_SIDE
+    window = shift_x // step * TILE_SIDE + shift_y // step
+    place_of = lax.broadcasted_iota(jnp.int32, (1, width), 1)
+    chosen = window == place_of % tile_count
+    spread = lax.broadcasted_iota(jnp.int32, (local, width), 1) // tile_count
+    spread = (spread == lax.broadcasted_iota(jnp.int32, (local, width), 0)).astype(jnp.float32).astype(jnp.bfloat16)
+    for at, part in ((0, first), (width, second)):
+        full = jnp.dot(part, spread, preferred_element_type=jnp.float32)
+        left_ref[:, at : at + width] = jnp.where(chosen, full, 0.0).astype(jnp.bfloat16)
+
     if other != strides:
         for at, old in moves:
             mixed_left[at : at + unit, :] = left_ref[old : old + unit, :]
@@ -229,7 +558,69 @@
     )
 
 
+def grad_by_columns(left_ref, res_ref, out_ref):
+    dims = (((0,), (0,)), ((), ()))
+    out_ref[...] = lax.dot_general(left_ref[...], res_ref[0], dims, preferred_element_type=jnp.float32).astype(
+        out_ref.dtype
+    )
+
+
+def grid_body(n, s_matrix, beam_weight, probe_shift, probe_cutoff, target, target_exp):
+    _, local, tile_count, pixels = s_matrix.shape
+    probes = probe_shift.shape[0]
+    unit = 2 * probes
+    rows = n * unit
+    block = rows // 8
+    width = local * tile_count
+    chunks = len(KINDS)
+    wide = pixels // chunks
+    pars = jnp.concatenate([probe_shift, probe_cutoff[:, None], target_exp[:, None]], axis=1)
+    pars = jnp.pad(jnp.concatenate([pars, pars], axis=0), ((0, 0), (0, 124)))
+    vmem = pl.BlockSpec(memory_space=pltpu.VMEM)
+    res, left = pl.pallas_call(
+        functools.partial(grid_kernel, n, local, tile_count, pixels),
+        out_shape=(
+            jax.ShapeDtypeStruct((chunks, 2, 2, 2, block, wide), jnp.bfloat16),
+            jax.ShapeDtypeStruct((rows, 2 * width), jnp.bfloat16),
+        ),
+        in_specs=[vmem, vmem, vmem, pl.BlockSpec(memory_space=pl.ANY)],
+        out_specs=(vmem, vmem),
+        scratch_shapes=[
+            pltpu.VMEM((rows, 128), jnp.int32),
+            pltpu.VMEM((2 * width, pixels), jnp.bfloat16),
+            pltpu.VMEM((chunks, 2, 2, 2, block, wide), jnp.float32),
+            pltpu.VMEM((chunks, 2, 2, 2, block, wide), jnp.bfloat16),
+            pltpu.VMEM((chunks, 2, 2, block, wide), jnp.bfloat16),
+            pltpu.VMEM((chunks, 2, block, wide), jnp.bfloat16),
+            pltpu.VMEM((chunks, 2, 2, block, wide), jnp.bfloat16),
+            pltpu.VMEM((chunks, 2, block, wide), jnp.bfloat16),
+            pltpu.SemaphoreType.DMA((n - 1,)),
+            pltpu.SemaphoreType.DMA((n - 1,)),
+            pltpu.SemaphoreType.DMA((chunks,)),
+            pltpu.SemaphoreType.DMA((chunks, 12)),
+            pltpu.SemaphoreType.DMA((chunks, len(NAMES))),
+        ],
+        compiler_params=pltpu.CompilerParams(
+            collective_id=0, has_side_effects=True, vmem_limit_bytes=60 * 2**20
+        ),
+    )(pars, beam_weight, target.reshape(unit, pixels), s_matrix.reshape(2 * width, pixels))
+    grad = pl.pallas_call(
+        grad_by_columns,
+        grid=(chunks,),
+        out_shape=jax.ShapeDtypeStruct((2 * width, pixels), jnp.bfloat16),
+        in_specs=[
+            pl.BlockSpec((rows, 2 * width), lambda i: (0, 0)),
+            pl.BlockSpec((1, rows, wide), lambda i: (i, 0, 0)),
+        ],
+        out_specs=pl.BlockSpec((2 * width, wide), lambda i: (0, i)),
+        compiler_params=pltpu.CompilerParams(vmem_limit_bytes=60 * 2**20),
+    )(left, res.reshape(chunks, rows, wide))
+    return grad.reshape(2, local, tile_count, pixels)
+
+
 def body(n, s_matrix, beam_weight, probe_shift, probe_cutoff, target, target_exp):
+    if n == 16:
+        return grid_body(n, s_matrix, beam_weight, probe_shift, probe_cutoff, target, target_exp)
     _, local, tile_count, pixels = s_matrix.shape
     probes = probe_shift.shape[0]
     strides, other = orders(n)

time: 60.7 us -> 63.2 us (1.041)
  Pallas kernels: 58.9 us -> 61.4 us
    pallas_call x2, Pallas kernels: 58.9 us -> 61.4 us  [the longest x1 50.7 us: grid_body(): pl.pallas_call(functools.partial(grid_kernel, n, local, tile_count, pixel...]
where the time goes in v1:
time: 63.2 us; the launch traced here: 62.9 us
  Pallas kernels  61.4 us (97%)
  other arithmetic  0.84 us (1%)
  local copies, waits for them, and re-layouts  0.69 us (1%)
    pallas_call x1, Pallas kernels, grid_body(): pl.pallas_call(functools.partial(grid_kernel, n, local, tile_count, pixel...  50.7 us
    pallas_call x1, Pallas kernels, grid_body(): pl.pallas_call(grad_by_columns, grid=(chunks,), out_shape=jax.ShapeDtypeS...  10.7 us

profile of v1, /device:TPU:0, one launch (start us, length us, event | category | flops | bytes accessed | tf_op | source)
XLA Modules:
  0.0 62.9 jit_solution(17834595967501066975)
XLA Ops:
  0.0 0.8 %add_add_fusion = s32[16,4]{0,1:T(4,128)S(1)} fusion(s32[8,1]{0,1:T(1,128)} %bitcast.9, s32[8,1]{0,1:T(1,128)} %bitcast.10, s32[8,2]{0,1:T(2,128)} %param.8), kind=kLoop, calls=%fused_computation | loop fusion | flops 320 | bytes 384 | tf_op jit(solution)/shard_map/concatenate | solution.py:578
  0.8 0.1 copy.10
  0.9 0.6 pad.4.par_ref
  1.5 50.7 %shard_map.64 = (bf16[8,2,2,2,32,512]{5,4,3,2,1,0:T(8,128)(2,1)}, bf16[256,2048]{1,0:T(8,128)(2,1)}) custom-call(s32[16,128]{1,0:T(8,128)} %pad.4.par_ref, f32[2,64]{1,0:T(2,128)} %weight_ref.1, bf16[16,4096]{1,0:T(8,128)(2,1)} %bitcast.8, bf16[2048,4096]{1,0:T(8,128)(2,1)} %bitcast.6), custom_call_target="tpu_custom_call" | custom-call | tf_op jit(solution)/shard_map/pallas_call | solution.py:580
  52.2 10.7 %shard_map.65 = bf16[2048,4096]{1,0:T(8,128)(2,1)} custom-call(bf16[256,2048]{1,0:T(8,128)(2,1)} %get-tuple-element.7.left_ref, bf16[8,256,512]{2,1,0:T(8,128)(2,1)} %bitcast.7), custom_call_target="tpu_custom_call" | custom-call | tf_op jit(solution)/shard_map/pallas_call | solution.py:607

commit v2 on v1

--- a/solution.py
+++ b/solution.py
@@ -26,10 +26,12 @@
 CORE_LAG = 0.9
 PRODUCT_US = 5.5
 ADD_US = 0.3
+GRADIENT_US = 10.0
+TURN_US = 0.5
 NAMES = ("r1", "r2", "r3f", "r3n", "r4", "ga", "gb", "gn1", "gn2", "gf1", "gf2", "ac")
 
 
-def steps_of(inner, kind):
+def steps_of(inner, kind, more):
     sums, spread = kind
     steps = [("M", (), (("c", "r1", 4),), 0, ())]
     if spread == "Y":
@@ -70,12 +72,18 @@
     else:
         steps.append(("A", ("gn1", "gn2", "gf1", "gf2"), (("c", "ac", 4),), 0, ()))
     steps.append(("E", ("ac",), (), 0, ()))
+    if more:
+        steps.append(("P0", (), (), 0, ("E",)))
+        steps.append(("P1", (), (), 0, ("P0",)))
+    else:
+        steps.append(("T0", (), (), 0, ("M",)))
+        steps.append(("T1", (), (), 0, ("T0",)))
     return steps
 
 
 def schedule(block_bytes):
     chunks = len(KINDS)
-    waiting = [[(k, step) for k in range(chunks) for step in steps_of(inner, KINDS[k])] for inner in (False, True)]
+    waiting = [[(k, step) for k in range(chunks) for step in steps_of(inner, KINDS[k], k < chunks - 1)] for inner in (False, True)]
     arrived, done = ({}, {}), ({}, {})
     free, links = [0.0, 0.0], {}
     order = ([], [])
@@ -86,15 +94,18 @@
                 name, needs, _, _, after = step
                 if name == "M" and k > 0 and (k - 1, "M") not in done[role]:
                     continue
+                if name == "P0" and (chunks - 1, "T1") not in done[role]:
+                    continue
                 if any((k, x) not in arrived[role] for x in needs) or any((k, x) not in done[role] for x in after):
                     continue
                 ready = max([free[role]] + [arrived[role][k, x] for x in needs])
-                rank = (ready, name == "M", k, role, name)
+                rank = (ready, name[0] in "MPT", name[0] in "PT", k, role, name)
                 if best is None or rank < best[0]:
                     best = (rank, role, k, step)
         (ready, *_), role, k, step = best
         name, _, sends, blocks, _ = step
-        end = ready + (PRODUCT_US if name == "M" else 0.02 * chunks + ADD_US * blocks) / chunks
+        cost = {"M": PRODUCT_US / chunks, "P": GRADIENT_US / 2 / chunks, "T": TURN_US}
+        end = ready + cost.get(name[0], 0.02 + ADD_US * blocks / chunks)
         free[role] = end
         done[role][k, name] = end
         waiting[role].remove((k, step))
@@ -109,15 +120,16 @@
 
 def grid_kernel(
     n, local, tile_count, pixels,
-    par_ref, weight_ref, target_ref, s_ref,
-    res_ref, left_ref,
-    pars, s_vmem, acc, sbuf, r1, r2, r3, r4,
+    shift_ref, cutoff_ref, exp_ref, weight_ref, target_hbm, s_ref,
+    grad_ref, res_ref, turned_ref,
+    raw, par_ref, target_ref, parts, left_ref, pars, acc, sbuf, r1, r2, r3, r4,
     par_send, par_recv, s_sem, send_sem, recv_sem,
 ):
     me = lax.axis_index("beam")
     unit = par_ref.shape[0]
     rows = n * unit
     width = local * tile_count
+    s_vmem = grad_ref
     chunks = len(KINDS)
     wide = pixels // chunks
     block = rows // 8
@@ -139,14 +151,25 @@
     loads = []
     for k in range(chunks):
         load = pltpu.make_async_copy(s_ref.at[:, columns(k)], s_vmem.at[:, columns(k)], s_sem.at[k])
-        load.start()
         loads.append(load)
-
+    target_load = pltpu.make_async_copy(target_hbm, target_ref, s_sem.at[chunks])
     barrier = pltpu.get_barrier_semaphore()
     for ahead in range(1, n):
         pl.semaphore_signal(
             barrier, inc=1, device_id={"beam": lax.rem(me + ahead, n)}, device_id_type=pl.DeviceIdType.MESH
         )
+    target_load.start()
+    for load in loads:
+        load.start()
+    probes = unit // 2
+    raw[...] = jnp.zeros_like(raw)
+    raw[0:2, 0:probes] = shift_ref[...]
+    raw[2:3, 0:probes] = cutoff_ref[...]
+    raw[3:4, 0:probes] = exp_ref[...]
+    table = raw[...].T[0:probes, :]
+    par_ref[...] = jnp.zeros_like(par_ref)
+    par_ref[0:probes, 0:8] = table
+    par_ref[probes:unit, 0:8] = table
     pl.semaphore_wait(barrier, n - 1)
 
     def remote(source, target, send_semaphore, recv_semaphore, peer):
@@ -198,6 +221,18 @@
     for at, part in ((0, first), (width, second)):
         full = jnp.dot(part, spread, preferred_element_type=jnp.float32)
         left_ref[:, at : at + width] = jnp.where(chosen, full, 0.0).astype(jnp.bfloat16)
+    parts[0] = first
+    parts[1] = second
+    target_load.wait()
+
+    def turn(part):
+        window_row = jnp.broadcast_to(window.astype(jnp.float32), (rows, 128)).T[0:1, :]
+        tile = lax.broadcasted_iota(jnp.int32, (width, 1), 0) % tile_count
+        beams = lax.broadcasted_iota(jnp.int32, (width, local), 0) // tile_count
+        beams = (beams == lax.broadcasted_iota(jnp.int32, (width, local), 1)).astype(jnp.float32).astype(jnp.bfloat16)
+        full = lax.dot_general(beams, parts[part], (((1,), (1,)), ((), ())), preferred_element_type=jnp.float32)
+        chosen_row = tile.astype(jnp.float32) == window_row
+        turned_ref[part * width : (part + 1) * width, :] = jnp.where(chosen_row, full, 0.0).astype(jnp.bfloat16)
 
     own = (me * unit // block // 4, me * unit // block // 2 % 2, me * unit // block % 2)
     own_rows = pl.ds(pl.multiple_of(me * unit % block, unit), unit)
@@ -327,6 +362,14 @@
                 send(k, "y", "gb", held, held)
             elif name == "E":
                 got(k, "ac", res_ref.at[k, 1 - core])
+            elif name in ("P0", "P1"):
+                half_rows = pl.ds(int(name[1]) * width, width)
+                product = jnp.dot(
+                    turned_ref[half_rows, :], res_ref[k].reshape(rows, wide), preferred_element_type=jnp.float32
+                )
+                grad_ref[half_rows, columns(k)] = low(product)
+            elif name in ("T0", "T1"):
+                turn(int(name[1]))
 
         for k, name in steps:
             take(k, name)
@@ -558,11 +601,23 @@
     )
 
 
-def grad_by_columns(left_ref, res_ref, out_ref):
-    dims = (((0,), (0,)), ((), ()))
-    out_ref[...] = lax.dot_general(left_ref[...], res_ref[0], dims, preferred_element_type=jnp.float32).astype(
-        out_ref.dtype
-    )
+def finish_kernel(done_ref, turned_ref, res_ref, out_ref, last, sem):
+    height = turned_ref.shape[0]
+    chunks, _, wide = res_ref.shape
+    ready = out_ref.shape[1] - wide
+    tall = height // 4
+    copies = []
+    for i in range(4):
+        at = pl.ds(i * tall, tall)
+        copies.append(pltpu.make_async_copy(done_ref.at[at, pl.ds(0, ready)], out_ref.at[at, pl.ds(0, ready)], sem.at[i]))
+        copies[-1].start()
+    for i in range(4):
+        at = pl.ds(i * tall, tall)
+        last[at, :] = jnp.dot(turned_ref[at, :], res_ref[chunks - 1], preferred_element_type=jnp.float32).astype(jnp.bfloat16)
+        copies.append(pltpu.make_async_copy(last.at[at, :], out_ref.at[at, pl.ds(ready, wide)], sem.at[4 + i]))
+        copies[-1].start()
+    for copy in copies:
+        copy.wait()
 
 
 def grid_body(n, s_matrix, beam_weight, probe_shift, probe_cutoff, target, target_exp):
@@ -574,20 +629,24 @@
     width = local * tile_count
     chunks = len(KINDS)
     wide = pixels // chunks
-    pars = jnp.concatenate([probe_shift, probe_cutoff[:, None], target_exp[:, None]], axis=1)
-    pars = jnp.pad(jnp.concatenate([pars, pars], axis=0), ((0, 0), (0, 124)))
     vmem = pl.BlockSpec(memory_space=pltpu.VMEM)
-    res, left = pl.pallas_call(
+    hbm = pl.BlockSpec(memory_space=pl.ANY)
+    done, res, turned = pl.pallas_call(
         functools.partial(grid_kernel, n, local, tile_count, pixels),
         out_shape=(
-            jax.ShapeDtypeStruct((chunks, 2, 2, 2, block, wide), jnp.bfloat16),
-            jax.ShapeDtypeStruct((rows, 2 * width), jnp.bfloat16),
+            pltpu.VMEM((2 * width, pixels), jnp.bfloat16),
+            pltpu.VMEM((chunks, 2, 2, 2, block, wide), jnp.bfloat16),
+            pltpu.VMEM((2 * width, rows), jnp.bfloat16),
         ),
-        in_specs=[vmem, vmem, vmem, pl.BlockSpec(memory_space=pl.ANY)],
-        out_specs=(vmem, vmem),
+        in_specs=[vmem, vmem, vmem, vmem, hbm, hbm],
+        out_specs=(vmem, vmem, vmem),
         scratch_shapes=[
+            pltpu.VMEM((8, 128), jnp.int32),
+            pltpu.VMEM((unit, 128), jnp.int32),
+            pltpu.VMEM((unit, pixels), jnp.bfloat16),
+            pltpu.VMEM((2, rows, local), jnp.bfloat16),
+            pltpu.VMEM((rows, 2 * width), jnp.bfloat16),
             pltpu.VMEM((rows, 128), jnp.int32),
-            pltpu.VMEM((2 * width, pixels), jnp.bfloat16),
             pltpu.VMEM((chunks, 2, 2, 2, block, wide), jnp.float32),
             pltpu.VMEM((chunks, 2, 2, 2, block, wide), jnp.bfloat16),
             pltpu.VMEM((chunks, 2, 2, block, wide), jnp.bfloat16),
@@ -596,25 +655,25 @@
             pltpu.VMEM((chunks, 2, block, wide), jnp.bfloat16),
             pltpu.SemaphoreType.DMA((n - 1,)),
             pltpu.SemaphoreType.DMA((n - 1,)),
-            pltpu.SemaphoreType.DMA((chunks,)),
+            pltpu.SemaphoreType.DMA((chunks + 1,)),
             pltpu.SemaphoreType.DMA((chunks, 12)),
             pltpu.SemaphoreType.DMA((chunks, len(NAMES))),
         ],
         compiler_params=pltpu.CompilerParams(
-            collective_id=0, has_side_effects=True, vmem_limit_bytes=60 * 2**20
+            collective_id=0, has_side_effects=True, vmem_limit_bytes=36 * 2**20
         ),
-    )(pars, beam_weight, target.reshape(unit, pixels), s_matrix.reshape(2 * width, pixels))
+    )(
+        probe_shift.T, probe_cutoff.reshape(1, probes), target_exp.reshape(1, probes), beam_weight,
+        target.reshape(unit, pixels), s_matrix.reshape(2 * width, pixels),
+    )
     grad = pl.pallas_call(
-        grad_by_columns,
-        grid=(chunks,),
+        finish_kernel,
         out_shape=jax.ShapeDtypeStruct((2 * width, pixels), jnp.bfloat16),
-        in_specs=[
-            pl.BlockSpec((rows, 2 * width), lambda i: (0, 0)),
-            pl.BlockSpec((1, rows, wide), lambda i: (i, 0, 0)),
-        ],
-        out_specs=pl.BlockSpec((2 * width, wide), lambda i: (0, i)),
-        compiler_params=pltpu.CompilerParams(vmem_limit_bytes=60 * 2**20),
-    )(left, res.reshape(chunks, rows, wide))
+        in_specs=[vmem, vmem, vmem],
+        out_specs=hbm,
+        scratch_shapes=[pltpu.VMEM((2 * width, wide), jnp.bfloat16), pltpu.SemaphoreType.DMA((8,))],
+        compiler_params=pltpu.CompilerParams(vmem_limit_bytes=8 * 2**20),
+    )(done, turned, res.reshape(chunks, rows, wide))
     return grad.reshape(2, local, tile_count, pixels)
 
 

time: 63.2 us -> 56.3 us (0.89)
  Pallas kernels: 61.4 us -> 56 us
  other arithmetic: 0.84 us -> 0 us
  local copies, waits for them, and re-layouts: 0.69 us -> 0 us
    pallas_call x1, Pallas kernels: 10.7 us -> 5.97 us  [grid_body(): pl.pallas_call(finish_kernel, out_shape=jax.ShapeDtypeStruct((2 * width,...]
    concatenate x1 -> x0, other arithmetic: 0.84 us -> none  [grid_body(): pars = jnp.pad(jnp.concatenate([pars, pars], axis=0), ((0, 0), (0, 124)))]
    pallas_call x1, Pallas kernels: 50.7 us -> 50 us  [grid_body(): pl.pallas_call(functools.partial(grid_kernel, n, local, tile_count, pixel...]
where the time goes in v2:
time: 56.3 us; the launch traced here: 56.1 us
  Pallas kernels  56 us (99%)
    pallas_call x1, Pallas kernels, grid_body(): pl.pallas_call(functools.partial(grid_kernel, n, local, tile_count, pixel...  50 us
    pallas_call x1, Pallas kernels, grid_body(): pl.pallas_call(finish_kernel, out_shape=jax.ShapeDtypeStruct((2 * width,...  5.97 us

profile of v2, /device:TPU:0, one launch (start us, length us, event | category | flops | bytes accessed | tf_op | source)
XLA Modules:
  0.0 56.1 jit_solution(5072880553818245016)
XLA Ops:
  0.0 50.0 %shard_map.64 = (bf16[2048,4096]{1,0:T(8,128)(2,1)S(1)}, bf16[8,2,2,2,32,512]{5,4,3,2,1,0:T(8,128)(2,1)S(1)}, bf16[2048,256]{1,0:T(8,128)(2,1)S(1)}) custom-call(s32[2,8]{1,0:T(2,128)} %bitcast.10, s32[1,8]{1,0:T(1,128)} %bitcast.11, s32[1,8]{1,0:T(1,128)} %bitcast.12, f32[2,64]{1,0:T(2,128)} %weight_ref.1, bf16[16,4096]{1,0:T(8,128)(2,1)} %bitcast.9, ...), custom_call_target="tpu_custom_call" | custom-call | tf_op jit(solution)/shard_map/pallas_call | solution.py:634
  50.0 6.0 %shard_map.65 = bf16[2048,4096]{1,0:T(8,128)(2,1)} custom-call(bf16[2048,4096]{1,0:T(8,128)(2,1)S(1)} %get-tuple-element.8.done_ref, bf16[2048,256]{1,0:T(8,128)(2,1)S(1)} %get-tuple-element.9.turned_ref, bf16[8,256,512]{2,1,0:T(8,128)(2,1)S(1)} %bitcast.7), custom_call_target="tpu_custom_call" | custom-call | tf_op jit(solution)/shard_map/pallas_call | solution.py:669

commit v3 on v2

--- a/solution.py
+++ b/solution.py
@@ -19,14 +19,15 @@
 MATMUL_COLUMNS = 512
 
 
-KINDS = ("YY",) * 8
+KINDS = ("YY", "ZY") + ("YY",) * 6
 LINK_RATE = 46.5e3
 CORE_RATE = 250e3
-LINK_LAG = 1.66
-CORE_LAG = 0.9
+LINK_LAG = 2.4
+CORE_LAG = 1.4
 PRODUCT_US = 5.5
 ADD_US = 0.3
 GRADIENT_US = 10.0
+LATE = 3
 TURN_US = 0.5
 NAMES = ("r1", "r2", "r3f", "r3n", "r4", "ga", "gb", "gn1", "gn2", "gf1", "gf2", "ac")
 
@@ -72,10 +73,10 @@
     else:
         steps.append(("A", ("gn1", "gn2", "gf1", "gf2"), (("c", "ac", 4),), 0, ()))
     steps.append(("E", ("ac",), (), 0, ()))
-    if more:
+    if more > 0:
         steps.append(("P0", (), (), 0, ("E",)))
         steps.append(("P1", (), (), 0, ("P0",)))
-    else:
+    elif more < 0:
         steps.append(("T0", (), (), 0, ("M",)))
         steps.append(("T1", (), (), 0, ("T0",)))
     return steps
@@ -83,7 +84,7 @@
 
 def schedule(block_bytes):
     chunks = len(KINDS)
-    waiting = [[(k, step) for k in range(chunks) for step in steps_of(inner, KINDS[k], k < chunks - 1)] for inner in (False, True)]
+    waiting = [[(k, step) for k in range(chunks) for step in steps_of(inner, KINDS[k], 1 - (k >= chunks - LATE) - (k == chunks - 1))] for inner in (False, True)]
     arrived, done = ({}, {}), ({}, {})
     free, links = [0.0, 0.0], {}
     order = ([], [])
@@ -122,11 +123,11 @@
     n, local, tile_count, pixels,
     shift_ref, cutoff_ref, exp_ref, weight_ref, target_hbm, s_ref,
     grad_ref, res_ref, turned_ref,
-    raw, par_ref, target_ref, parts, left_ref, pars, acc, sbuf, r1, r2, r3, r4,
+    raw, par_ref, scale_ref, flat, mix, target_ref, parts, left_ref, pars, acc, sbuf, r1, r2, r3, r4,
     par_send, par_recv, s_sem, send_sem, recv_sem,
 ):
     me = lax.axis_index("beam")
-    unit = par_ref.shape[0]
+    unit = scale_ref.shape[0]
     rows = n * unit
     width = local * tile_count
     s_vmem = grad_ref
@@ -166,10 +167,14 @@
     raw[0:2, 0:probes] = shift_ref[...]
     raw[2:3, 0:probes] = cutoff_ref[...]
     raw[3:4, 0:probes] = exp_ref[...]
-    table = raw[...].T[0:probes, :]
-    par_ref[...] = jnp.zeros_like(par_ref)
-    par_ref[0:probes, 0:8] = table
-    par_ref[probes:unit, 0:8] = table
+    scale = jnp.exp2(raw[...].T[0:probes, 3:4].astype(jnp.float32))
+    scale_ref[0:probes, :] = jnp.broadcast_to(scale, (probes, 128))
+    scale_ref[probes:unit, :] = jnp.broadcast_to(scale, (probes, 128))
+    table = raw[...]
+    packed = table[0:1, :]
+    for k in range(1, 4):
+        packed = packed + pltpu.roll(table, k * probes, 1)[k : k + 1, :]
+    par_ref[0] = packed
     pl.semaphore_wait(barrier, n - 1)
 
     def remote(source, target, send_semaphore, recv_semaphore, peer):
@@ -182,24 +187,29 @@
             device_id_type=pl.DeviceIdType.MESH,
         )
 
-    mine = pl.ds(pl.multiple_of(me * unit, unit), unit)
-    pars[mine, :] = par_ref[...]
+    pars[me] = par_ref[0]
     asked = [
-        remote(par_ref, pars.at[mine, :], par_send.at[ahead - 1], par_recv.at[ahead - 1], lax.rem(me + ahead, n))
+        remote(par_ref.at[0], pars.at[me], par_send.at[ahead - 1], par_recv.at[ahead - 1], lax.rem(me + ahead, n))
         for ahead in range(1, n)
     ]
     for copy in asked:
         copy.start()
     for copy in asked:
         copy.wait_recv()
+    for at in range(n):
+        flat[at : at + 1, :] = pars[at]
+    turned = flat[...].T
+
+    def column(k):
+        return jnp.concatenate([turned[k * probes : (k + 1) * probes, at : at + 1] for at in range(n)], axis=0)
 
     half = SIDE // 2
     beam = me * local + lax.broadcasted_iota(jnp.int32, (1, local), 1)
     freq_x = beam % SIDE - half
     freq_y = beam // SIDE - half
-    shift_x = pars[:, 0:1]
-    shift_y = pars[:, 1:2]
-    cutoff = pars[:, 2:3]
+    shift_x = column(0)
+    shift_y = column(1)
+    cutoff = column(2)
     ramp = (freq_x * shift_x + freq_y * shift_y) % GRID
     phase = ramp.astype(jnp.float32) * (TWO_PI / GRID)
     inside = (freq_x * freq_x + freq_y * freq_y) <= cutoff
@@ -207,13 +217,17 @@
     sine = jnp.sin(phase)
     w_real = weight_ref[0:1, :]
     w_imag = weight_ref[1:2, :]
-    c_real = jnp.where(inside, w_real * cosine + w_imag * sine, 0.0)
-    c_imag = jnp.where(inside, w_imag * cosine - w_real * sine, 0.0)
-    is_real = lax.broadcasted_iota(jnp.int32, (rows, 1), 0) % unit < unit // 2
-    first = jnp.where(is_real, c_real, c_imag).astype(jnp.bfloat16)
-    second = jnp.where(is_real, -c_imag, c_real).astype(jnp.bfloat16)
+    c_real = jnp.where(inside, w_real * cosine + w_imag * sine, 0.0).reshape(n, probes, local)
+    c_imag = jnp.where(inside, w_imag * cosine - w_real * sine, 0.0).reshape(n, probes, local)
+    mix[0, :, 0] = c_real
+    mix[0, :, 1] = c_imag
+    mix[1, :, 0] = -c_imag
+    mix[1, :, 1] = c_real
+    first = mix[0].reshape(rows, local).astype(jnp.bfloat16)
+    second = mix[1].reshape(rows, local).astype(jnp.bfloat16)
     step = GRID // TILE_SIDE
-    window = shift_x // step * TILE_SIDE + shift_y // step
+    window = (shift_x // step * TILE_SIDE + shift_y // step).reshape(n, probes, 1)
+    window = jnp.concatenate([window, window], axis=1).reshape(rows, 1)
     place_of = lax.broadcasted_iota(jnp.int32, (1, width), 1)
     chosen = window == place_of % tile_count
     spread = lax.broadcasted_iota(jnp.int32, (local, width), 1) // tile_count
@@ -273,7 +287,7 @@
                 loads[k].wait()
                 product = jnp.dot(left_ref[...], s_vmem[:, columns(k)], preferred_element_type=jnp.float32)
                 acc[k] = product.reshape(2, 2, 2, block, wide)
-                goal = target_ref[:, columns(k)].astype(jnp.float32) * jnp.exp2(par_ref[:, 3:4].astype(jnp.float32))
+                goal = target_ref[:, columns(k)].astype(jnp.float32) * scale_ref[:, 0:1]
                 acc[(k, *own, own_rows)] = acc[(k, *own, own_rows)] - goal
                 sbuf[k, 1 - core] = low(acc[k, 1 - core])
                 send(k, "c", "r1", sbuf.at[k, 1 - core], r1.at[k])
@@ -363,11 +377,15 @@
             elif name == "E":
                 got(k, "ac", res_ref.at[k, 1 - core])
             elif name in ("P0", "P1"):
-                half_rows = pl.ds(int(name[1]) * width, width)
-                product = jnp.dot(
-                    turned_ref[half_rows, :], res_ref[k].reshape(rows, wide), preferred_element_type=jnp.float32
-                )
-                grad_ref[half_rows, columns(k)] = low(product)
+                tall = width // 2
+
+                def part_of(i, carry):
+                    at = pl.ds(pl.multiple_of((2 * int(name[1]) + i) * tall, tall), tall)
+                    held = res_ref[k].reshape(rows, wide)
+                    grad_ref[at, columns(k)] = low(jnp.dot(turned_ref[at, :], held, preferred_element_type=jnp.float32))
+                    return carry
+
+                lax.fori_loop(0, 2, part_of, 0)
             elif name in ("T0", "T1"):
                 turn(int(name[1]))
 
@@ -604,7 +622,7 @@
 def finish_kernel(done_ref, turned_ref, res_ref, out_ref, last, sem):
     height = turned_ref.shape[0]
     chunks, _, wide = res_ref.shape
-    ready = out_ref.shape[1] - wide
+    ready = out_ref.shape[1] - wide * LATE
     tall = height // 4
     copies = []
     for i in range(4):
@@ -613,8 +631,11 @@
         copies[-1].start()
     for i in range(4):
         at = pl.ds(i * tall, tall)
-        last[at, :] = jnp.dot(turned_ref[at, :], res_ref[chunks - 1], preferred_element_type=jnp.float32).astype(jnp.bfloat16)
-        copies.append(pltpu.make_async_copy(last.at[at, :], out_ref.at[at, pl.ds(ready, wide)], sem.at[4 + i]))
+        for k in range(LATE):
+            held = res_ref[chunks - LATE + k]
+            product = jnp.dot(turned_ref[at, :], held, preferred_element_type=jnp.float32)
+            last[at, k * wide : (k + 1) * wide] = product.astype(jnp.bfloat16)
+        copies.append(pltpu.make_async_copy(last.at[at, :], out_ref.at[at, pl.ds(ready, wide * LATE)], sem.at[4 + i]))
         copies[-1].start()
     for copy in copies:
         copy.wait()
@@ -642,11 +663,14 @@
         out_specs=(vmem, vmem, vmem),
         scratch_shapes=[
             pltpu.VMEM((8, 128), jnp.int32),
-            pltpu.VMEM((unit, 128), jnp.int32),
+            pltpu.VMEM((1, 1, 128), jnp.int32),
+            pltpu.VMEM((unit, 128), jnp.float32),
+            pltpu.VMEM((n, 128), jnp.int32),
+            pltpu.VMEM((2, n, 2, probes, local), jnp.float32),
             pltpu.VMEM((unit, pixels), jnp.bfloat16),
             pltpu.VMEM((2, rows, local), jnp.bfloat16),
             pltpu.VMEM((rows, 2 * width), jnp.bfloat16),
-            pltpu.VMEM((rows, 128), jnp.int32),
+            pltpu.VMEM((n, 1, 128), jnp.int32),
             pltpu.VMEM((chunks, 2, 2, 2, block, wide), jnp.float32),
             pltpu.VMEM((chunks, 2, 2, 2, block, wide), jnp.bfloat16),
             pltpu.VMEM((chunks, 2, 2, block, wide), jnp.bfloat16),
@@ -671,14 +695,14 @@
         out_shape=jax.ShapeDtypeStruct((2 * width, pixels), jnp.bfloat16),
         in_specs=[vmem, vmem, vmem],
         out_specs=hbm,
-        scratch_shapes=[pltpu.VMEM((2 * width, wide), jnp.bfloat16), pltpu.SemaphoreType.DMA((8,))],
+        scratch_shapes=[pltpu.VMEM((2 * width, wide * LATE), jnp.bfloat16), pltpu.SemaphoreType.DMA((8,))],
         compiler_params=pltpu.CompilerParams(vmem_limit_bytes=8 * 2**20),
     )(done, turned, res.reshape(chunks, rows, wide))
     return grad.reshape(2, local, tile_count, pixels)
 
 
 def body(n, s_matrix, beam_weight, probe_shift, probe_cutoff, target, target_exp):
-    if n == 16:
+    if n == 16 and probe_shift.shape[0] == 8:
         return grid_body(n, s_matrix, beam_weight, probe_shift, probe_cutoff, target, target_exp)
     _, local, tile_count, pixels = s_matrix.shape
     probes = probe_shift.shape[0]

time: 56.3 us -> 52.1 us (0.925)
  Pallas kernels: 56 us -> 51.8 us
    pallas_call x1, Pallas kernels: 50 us -> 45.8 us  [grid_body(): pl.pallas_call(functools.partial(grid_kernel, n, local, tile_count, pixel...]
where the time goes in v3:
time: 52.1 us; the launch traced here: 51.9 us
  Pallas kernels  51.8 us (99%)
    pallas_call x1, Pallas kernels, grid_body(): pl.pallas_call(functools.partial(grid_kernel, n, local, tile_count, pixel...  45.8 us
    pallas_call x1, Pallas kernels, grid_body(): pl.pallas_call(finish_kernel, out_shape=jax.ShapeDtypeStruct((2 * width,...  5.95 us

profile of v3, /device:TPU:0, one launch (start us, length us, event | category | flops | bytes accessed | tf_op | source)
XLA Modules:
  0.0 51.9 jit_solution(9853568418153982620)
XLA Ops:
  0.0 45.8 %shard_map.64 = (bf16[2048,4096]{1,0:T(8,128)(2,1)S(1)}, bf16[8,2,2,2,32,512]{5,4,3,2,1,0:T(8,128)(2,1)S(1)}, bf16[2048,256]{1,0:T(8,128)(2,1)S(1)}) custom-call(s32[2,8]{1,0:T(2,128)} %bitcast.10, s32[1,8]{1,0:T(1,128)} %bitcast.11, s32[1,8]{1,0:T(1,128)} %bitcast.12, f32[2,64]{1,0:T(2,128)} %weight_ref.1, bf16[16,4096]{1,0:T(8,128)(2,1)} %bitcast.9, ...), custom_call_target="tpu_custom_call" | custom-call | tf_op jit(solution)/shard_map/pallas_call | solution.py:655
  45.8 6.0 %shard_map.65 = bf16[2048,4096]{1,0:T(8,128)(2,1)} custom-call(bf16[2048,4096]{1,0:T(8,128)(2,1)S(1)} %get-tuple-element.8.done_ref, bf16[2048,256]{1,0:T(8,128)(2,1)S(1)} %get-tuple-element.9.turned_ref, bf16[8,256,512]{2,1,0:T(8,128)(2,1)S(1)} %bitcast.7), custom_call_target="tpu_custom_call" | custom-call | tf_op jit(solution)/shard_map/pallas_call | solution.py:693
